TPU v7x, 512 devices: a whole 4x4x16 slice. The times are simulated.
512 devices in a mesh: pipe: 8 (over y_lo, x), dp: 64 (over z, y_hi, core).
Axes of the slice: x: 4, y: 4 (y_hi: 2, y_lo: 2; y = y_hi * 2 + y_lo), z: 16, core: 2. Of those that a mesh axis runs over, the one named last changes fastest.
Arguments:
- visual_fragments: bfloat16 [8, 64, 64, 1152], P(None, 'dp'), may hold values from -6 to 6
- widening_kernel: bfloat16 [8, 1152, 2176], P('pipe', None, 'dp'), may hold values from -0.1875 to 0.1875
- narrowing_kernel: bfloat16 [8, 2176, 1152], P('pipe', 'dp'), may hold values from -0.125 to 0.125
- caption_outputs: bfloat16 [4608, 1152], P(('pipe', 'dp')), may hold values from -6 to 6
- earlier_averaged: float32 [4096, 1152], P(('pipe', 'dp')), may hold values from -6 to 6
- match_targets: int32 [4608], replicated, may hold values from 0 to 4607, each once
- score_scaling: float32 [1], replicated, may hold values from 5 to 15
- score_shift: float32 [1], replicated, may hold values from -4 to -2
Outputs:
- image_grad: float32 [4608, 1152], P(('pipe', 'dp'))
- text_grad: float32 [4608, 1152], P(('pipe', 'dp'))
Inputs may be any that keep to these rules, and one draw needn't show every extreme that they name: match_targets is a permutation: every text is the positive of exactly one image.
All inputs are finite; a program needn't handle non-finite values.
Results may differ from a plain program's by a relative error of at most 0.017.
Values may be sent and summed in bfloat16 or wider, within the bound.
No kernel may reach another device: no remote copies, remote signals or barrier semaphores. Data moves between devices by JAX's collectives and lax.ppermute only.
A program may use at most 128 MiB of HBM per device.

v0:
```python
import jax
import jax.numpy as jnp
from jax import lax
from jax.sharding import PartitionSpec as P


def from_behind(value, axis, steps):
    count = lax.axis_size(axis)
    pairs = [(source, (source + steps) % count) for source in range(count)]
    return lax.ppermute(value, axis, pairs)


def layer_norm(hidden_rows):
    values = hidden_rows.astype(jnp.float32)
    centre = jnp.mean(values, axis=-1, keepdims=True)
    shifted = values - centre
    variance = jnp.mean(shifted * shifted, axis=-1, keepdims=True)
    return (shifted * lax.rsqrt(variance + 1e-06)).astype(jnp.bfloat16)


def section_block(hidden_rows, w_up, w_down):
    normed = layer_norm(hidden_rows)
    pre_act = jnp.dot(normed, w_up, preferred_element_type=jnp.float32)
    activated = jax.nn.gelu(pre_act, approximate=True).astype(jnp.bfloat16)
    updated = hidden_rows.astype(jnp.float32) + jnp.dot(
        activated, w_down, preferred_element_type=jnp.float32
    )
    return updated.astype(jnp.bfloat16)


def unit_rows(values):
    values = values.astype(jnp.float32)
    total = jnp.sum(values * values, axis=-1, keepdims=True)
    return (values * lax.rsqrt(total + 1e-06)).astype(jnp.bfloat16)


def coupling_factors(
    picture_group, source_caption_tile, match_entries, target_tile, sharpness_factor, shift_addend
):
    similarity_scores = (
        sharpness_factor
        * jnp.dot(picture_group, source_caption_tile.T, preferred_element_type=jnp.float32)
        + shift_addend
    )
    matching_couples = match_entries[:, None] == target_tile[None, :]
    coefficient_grid = jnp.where(
        matching_couples,
        -sharpness_factor * jax.nn.sigmoid(-similarity_scores),
        sharpness_factor * jax.nn.sigmoid(similarity_scores),
    )
    return coefficient_grid.astype(jnp.bfloat16)


def body(
    visual_fragments,
    widening_kernel,
    narrowing_kernel,
    caption_outputs,
    earlier_averaged,
    match_targets,
    score_scaling,
    score_shift,
):
    sections = lax.axis_size("pipe")
    section_id = lax.axis_index("pipe")
    data_count = lax.axis_size("dp")
    data_id = lax.axis_index("dp")
    micros, img_mb, patch_count, model_width = visual_fragments.shape
    tok_rows = img_mb * patch_count
    sharpness_factor = score_scaling[0]
    shift_addend = score_shift[0]
    caption_vectors = unit_rows(caption_outputs)
    up_full, down_full = (
        lax.all_gather(widening_kernel, "dp", axis=2, tiled=True),
        lax.all_gather(narrowing_kernel, "dp", axis=1, tiled=True),
    )
    up_full = up_full[0]
    down_full = down_full[0]
    panels = visual_fragments.reshape(micros, tok_rows, model_width)

    def advance(step, current):
        pick = jnp.clip(sections - 1 - step, 0, micros - 1)
        incoming = lax.dynamic_index_in_dim(panels, pick, 0, keepdims=False)
        current = jnp.where((section_id == 0) & (step < sections), incoming, current)
        active = (step >= section_id) & (step - section_id < sections)
        current = lax.cond(
            active,
            lambda carried: section_block(carried, up_full, down_full),
            lambda carried: carried,
            current,
        )
        return from_behind(current, "pipe", 1)

    finished = lax.fori_loop(
        0, 2 * sections - 1, advance, jnp.zeros((tok_rows, model_width), jnp.bfloat16)
    )
    pooled = jnp.mean(
        finished.astype(jnp.float32).reshape(img_mb, patch_count, model_width), axis=1
    )
    picture_vectors = jnp.concatenate([unit_rows(pooled), unit_rows(earlier_averaged)], axis=0)
    rows_dev = picture_vectors.shape[0]
    row_width = data_count * rows_dev
    text_row_block = lax.all_gather(caption_vectors, "dp", axis=0, tiled=True)
    image_column_block = lax.all_gather(picture_vectors, "pipe", axis=0, tiled=True)
    label_table = match_targets.reshape(sections, row_width)
    label_columns = lax.dynamic_slice_in_dim(label_table, data_id * rows_dev, rows_dev, 1).reshape(
        -1
    )
    column_text_block = section_id * row_width + jnp.arange(row_width, dtype=jnp.int32)
    grid_weights = coupling_factors(
        image_column_block,
        text_row_block,
        label_columns,
        column_text_block,
        sharpness_factor,
        shift_addend,
    )
    block = grid_weights
    image_grad = lax.psum_scatter(
        jnp.dot(block, text_row_block, preferred_element_type=jnp.float32).astype(jnp.bfloat16),
        "pipe",
        scatter_dimension=0,
        tiled=True,
    ).astype(jnp.float32)
    block = grid_weights
    text_grad = lax.psum_scatter(
        jnp.dot(block.T, image_column_block, preferred_element_type=jnp.float32),
        "dp",
        scatter_dimension=0,
        tiled=True,
    )
    return (image_grad, text_grad)


def solution(mesh):
    placed = (
        P(None, "dp", None, None),
        P("pipe", None, "dp"),
        P("pipe", "dp", None),
        P(("pipe", "dp"), None),
        P(("pipe", "dp"), None),
        P(),
        P(),
        P(),
    )
    return jax.shard_map(
        body,
        mesh=mesh,
        in_specs=placed,
        out_specs=(P(("pipe", "dp"), None), P(("pipe", "dp"), None)),
        check_vma=False,
    )
```

profile of v0, /device:TPU:1, one launch (start us, length us, event | category | flops | bytes accessed | tf_op | source)
XLA Modules:
  0.0 1396.2 jit_solution(13821860944951176592)
XLA Ops:
  17.2 145.3 %all-gather.10.cloned.1.call-done = bf16[64,9,1152]{2,1,0:T(8,128)(2,1)} async-done(((bf16[1,9,1152]{2,1,0:T(8,128)(2,1)}), bf16[64,9,1152]{2,1,0:T(8,128)(2,1)}) %all-gather.10.cloned.1.call-update) | async-done | bytes 1327120 | tf_op jit(solution)/shard_map/all_gather | solution.py:103
  165.1 165.6 %all-gather.8.cloned.1.call-done = bf16[1,2176,1152]{2,0,1:T(2,128)(2,1)} async-done(((bf16[1,34,1152]{2,0,1:T(2,128)(2,1)}), bf16[1,2176,1152]{2,0,1:T(2,128)(2,1)}) %all-gather.8.cloned.1.call-update) | async-done | bytes 5013520 | tf_op jit(solution)/shard_map/all_gather | solution.py:75
  330.7 6.9 copy.20
  337.6 161.9 %all-gather.6.cloned.1.call-done = bf16[1,1152,2176]{1,0,2:T(2,128)(2,1)} async-done(((bf16[1,1152,34]{1,0,2:T(2,128)(2,1)}), bf16[1,1152,2176]{1,0,2:T(2,128)(2,1)}) %all-gather.6.cloned.1.call-update) | async-done | bytes 5013520 | tf_op jit(solution)/shard_map/all_gather | solution.py:74
  499.5 22.0 %copy.16 = bf16[1,1152,2176]{2,1,0:T(8,128)(2,1)} copy(bf16[1,1152,2176]{1,0,2:T(2,128)(2,1)} %all-gather.6.cloned.1.call-done) | data formatting | bytes 10027008 | tf_op jit(solution)/shard_map/all_gather | solution.py:74
  521.5 213.1 %while.14 = (s32[]{:T(128)}, bf16[64,1152]{1,0:T(8,128)(2,1)S(1)}, s32[]{:T(128)}, pred[]{:T(512)}, bf16[8,64,1152]{2,1,0:T(8,128)(2,1)}, /*index=5*/bf16[1152,2...) while((s32[]{:T(128)}, bf16[64,1152]{1,0:T(8,128)(2,1)S(1)}, ...), condition=%wide.region_5.6_spmd, body=%wide.region_0.5_spmd.sunk | while | flops 644014144 | bytes 11946512 | solution.py:94
  522.5 6.1 conditional.2
  530.5 7.3 collective-permute-done
  538.7 6.1 conditional.2
  553.7 6.1 conditional.2
  568.7 6.1 conditional.2
  583.7 6.1 conditional.2
  598.8 6.1 conditional.2
  613.8 6.1 conditional.2
  628.8 6.1 conditional.2
  656.8 10.0 collective-permute-done
  669.7 10.0 collective-permute-done
  682.6 10.0 collective-permute-done
  695.5 11.4 collective-permute-done
  709.9 11.8 collective-permute-done
  724.5 10.1 collective-permute-done
  736.0 22.1 %all-gather = bf16[8,9,1152]{2,1,0:T(8,128)(2,1)S(1)} all-gather(bf16[1,9,1152]{2,1,0:T(8,128)(2,1)S(1)} %maximum_bitcast_fusion), channel_id=1, replica_groups=mesh['pipe'=8,'dp'=64] {'pipe'}, dimensions={0}, use_global_device_ids=true | all-gather | bytes 186624 | tf_op jit(solution)/shard_map/all_gather | solution.py:104
  765.9 91.5 %all-reduce.5.cloned.1.call-done = bf16[72,1152]{1,0:T(8,128)(2,1)} async-done(((bf16[72,1152]{1,0:T(8,128)(2,1)}), bf16[72,1152]{1,0:T(8,128)(2,1)}) %all-reduce.5.cloned.1.call-update) | async-done | bytes 165904
  858.8 529.3 %all-reduce.7.cloned.1.call-done = f32[576,1152]{1,0:T(8,128)} async-done(((f32[576,1152]{1,0:T(8,128)}), f32[576,1152]{1,0:T(8,128)}) %all-reduce.7.cloned.1.call-update) | async-done | bytes 2654224
  (130 shorter events, 163.3 us)
Async XLA Ops:
  7.2 155.3 %all-gather.10.cloned.1.call-start = ((), (), s32[]{:S(2)}) async-start(), calls=%async_computation.2 | async-start | bytes 2396160 | tf_op jit(solution)/shard_map/all_gather | solution.py:103
  9.6 321.1 %all-gather.8.cloned.1.call-start = ((), (), s32[]{:S(2)}) async-start(), calls=%async_computation.1 | async-start | bytes 10183680 | tf_op jit(solution)/shard_map/all_gather | solution.py:75
  11.4 488.1 %all-gather.6.cloned.1.call-start = ((), (), s32[]{:S(2)}) async-start(), calls=%async_computation | async-start | bytes 10183680 | tf_op jit(solution)/shard_map/all_gather | solution.py:74
  13.1 844.3 %all-reduce.5.cloned.1.call-start = ((), (), s32[]{:S(2)}) async-start(), calls=%async_computation.3 | async-start | bytes 331776
  528.6 9.2 collective-permute-start
  544.8 8.0 collective-permute-start
  559.8 8.0 collective-permute-start
  574.8 8.0 collective-permute-start
  589.8 8.0 collective-permute-start
  604.9 8.0 collective-permute-start
  619.9 8.0 collective-permute-start
  634.9 8.0 collective-permute-start
  643.8 10.1 collective-permute-start
  654.9 12.0 collective-permute-start
  667.8 12.0 collective-permute-start
  680.7 12.0 collective-permute-start
  693.6 13.4 collective-permute-start
  707.9 13.7 collective-permute-start
  722.6 12.0 collective-permute-start
  759.9 628.2 %all-reduce.7.cloned.1.call-start = ((), (), s32[]{:S(2)}) async-start(), calls=%async_computation.4 | async-start | bytes 5308416
Sparse Core Ops, SparseCore 0:
  11.8 150.6 all-gather.9
  165.7 164.9 all-gather.7
  333.9 165.5 all-gather.5
  760.0 97.3 all-reduce.4
  860.4 527.6 all-reduce.6
where the time goes:
time: 1400 us
  waiting for transfers between devices  1210 us (86%)
  matrix products  49.4 us (4%)
  local copies, waits for them, and re-layouts  40.1 us (3%)
  starting transfers between devices  33 us (2%)
  other arithmetic  22.9 us (2%)
  blocking collectives  22.1 us (2%)
  between operations  17.1 us (1%)
    unnamed x7, waiting for transfers between devices  621 us
    all_gather x1, waiting for transfers between devices, body(): lax.all_gather(narrowing_kernel, 'dp', axis=1, tiled=True)  166 us
    all_gather x1, waiting for transfers between devices, body(): lax.all_gather(widening_kernel, 'dp', axis=2, tiled=True)  162 us
    all_gather x1, waiting for transfers between devices, body(): text_row_block = lax.all_gather(caption_vectors, 'dp', axis=0, tiled=True)  145 us
    ppermute x15, waiting for transfers between devices, from_behind(): return lax.ppermute(value, axis, pairs)  117 us
    dot_general x8, matrix products, section_block(): jnp.dot(activated, w_down, preferred_element_type=jnp.float32)  45.6 us
    ppermute x15, starting transfers between devices, from_behind(): return lax.ppermute(value, axis, pairs)  32.8 us
  transfers between devices with their start and end apart: 20, of which 20 were waited for; matrix products, arithmetic and copies ran while one was open for 2% of the time, Pallas kernels for 0%

commit v1 on v0

v1 whole, which is shorter than its diff:
```python
import functools

import jax
import jax.numpy as jnp
from jax import lax
from jax.experimental import pallas as pl
from jax.experimental.pallas import tpu as pltpu
from jax.sharding import Mesh, PartitionSpec as P

STAGE_GAP = 2
GROUP = 1
PLANE = ("pipe", "yh", "core")
EVERY = ("pipe", "z", "yh", "core")


def unit_rows(values):
    values = values.astype(jnp.float32)
    total = jnp.sum(values * values, axis=-1, keepdims=True)
    return (values * lax.rsqrt(total + 1e-06)).astype(jnp.bfloat16)


def share_rows(rows, axes, count):
    copies = jnp.broadcast_to(rows[None], (count,) + rows.shape)
    return lax.all_to_all(copies, axes, 0, 0)


def swap(value, axis):
    return lax.ppermute(value, axis, [(0, 1), (1, 0)])


def stage_kernel(first_ref, panel_ref, carried_ref, up_a, down_a, up_b, down_b, out_ref, pooled_ref, normed_ref, hidden_ref, act_ref, *, take, wide, narrow):
    rows, width = carried_ref.shape
    if take == "panel":
        hidden = panel_ref[0].astype(jnp.float32)
    elif take == "carried":
        hidden = carried_ref[...].astype(jnp.float32)
    else:
        fresh = panel_ref[0].astype(jnp.float32)
        moved = carried_ref[...].astype(jnp.float32)
        hidden = jnp.where(first_ref[0] == 1, fresh, moved)
    centre = jnp.mean(hidden, axis=-1, keepdims=True)
    shifted = hidden - centre
    variance = jnp.mean(shifted * shifted, axis=-1, keepdims=True)
    normed = (shifted * lax.rsqrt(variance + 1e-06)).astype(jnp.bfloat16)
    normed_ref[...] = normed
    units = up_a.shape[0]
    for half, up_ref in enumerate((up_a, up_b)):

        @pl.loop(0, units // wide)
        def _(index, half=half, up_ref=up_ref):
            at = pl.multiple_of(index * wide, wide)
            pre_act = lax.dot_general(
                normed_ref[...],
                up_ref[pl.ds(at, wide), :],
                (((1,), (1,)), ((), ())),
                preferred_element_type=jnp.float32,
            )
            to = pl.multiple_of(half * units + index * wide, 128)
            act_ref[:, pl.ds(to, wide)] = jax.nn.gelu(pre_act, approximate=True).astype(jnp.bfloat16)

    hidden_ref[...] = hidden.astype(jnp.bfloat16)

    @pl.loop(0, width // narrow)
    def _(index):
        at = pl.multiple_of(index * narrow, narrow)
        total = hidden_ref[:, pl.ds(at, narrow)].astype(jnp.float32)
        total += jnp.dot(act_ref[:, :units], down_a[:, pl.ds(at, narrow)], preferred_element_type=jnp.float32)
        total += jnp.dot(act_ref[:, units:], down_b[:, pl.ds(at, narrow)], preferred_element_type=jnp.float32)
        updated = total.astype(jnp.bfloat16)
        out_ref[:, pl.ds(at, narrow)] = updated
        images = pooled_ref.shape[0]
        for image in range(images):
            patches = rows // images
            mean = jnp.mean(updated[image * patches : (image + 1) * patches].astype(jnp.float32), axis=0, keepdims=True)
            pooled_ref[image : image + 1, pl.ds(at, narrow)] = mean


def stage(first, panels, pick, carried, weights, images, take, wide=384, narrow=384):
    rows, width = carried.shape
    units = weights[0].shape[0]
    whole = pl.BlockSpec(memory_space=pltpu.VMEM)
    return pl.pallas_call(
        functools.partial(stage_kernel, take=take, wide=wide, narrow=narrow),
        grid_spec=pltpu.PrefetchScalarGridSpec(
            num_scalar_prefetch=1,
            grid=(1,),
            in_specs=[
                pl.BlockSpec((1, rows, width), lambda i, first: (pick, 0, 0)),
                pl.BlockSpec((rows, width), lambda i, first: (0, 0)),
                whole,
                whole,
                whole,
                whole,
            ],
            out_specs=[
                pl.BlockSpec((rows, width), lambda i, first: (0, 0)),
                pl.BlockSpec((images, width), lambda i, first: (0, 0)),
            ],
            scratch_shapes=[
                pltpu.VMEM((rows, width), jnp.bfloat16),
                pltpu.VMEM((rows, width), jnp.bfloat16),
                pltpu.VMEM((rows, 2 * units), jnp.bfloat16),
            ],
        ),
        out_shape=[
            jax.ShapeDtypeStruct((rows, width), jnp.bfloat16),
            jax.ShapeDtypeStruct((images, width), jnp.float32),
        ],
        compiler_params=pltpu.CompilerParams(vmem_limit_bytes=24 << 20),
        cost_estimate=pl.CostEstimate(
            flops=8 * rows * width * units,
            bytes_accessed=8 * width * units,
            transcendentals=2 * rows * units,
        ),
        name="stage",
    )(first, panels, carried, *weights)


def pair_weights(images, texts, targets, columns, scale, shift):
    scores = scale * lax.dot_general(
        images, texts, (((1,), (1,)), ((), ())), preferred_element_type=jnp.float32
    ) + shift
    grid = jnp.where(
        targets[:, None] == columns[None, :],
        -scale * jax.nn.sigmoid(-scores),
        scale * jax.nn.sigmoid(scores),
    )
    return grid.astype(jnp.bfloat16)


def across(grid, other):
    return lax.dot_general(grid, other, (((0,), (0,)), ((), ())), preferred_element_type=jnp.float32)


def body(
    visual_fragments,
    widening_kernel,
    narrowing_kernel,
    caption_outputs,
    earlier_averaged,
    match_targets,
    score_scaling,
    score_shift,
):
    stages = lax.axis_size("pipe")
    depth = lax.axis_size("z")
    stage_id = lax.axis_index("pipe")
    z_id = lax.axis_index("z")
    around = lax.axis_size("yh") * lax.axis_size("core")
    around_id = lax.axis_index("yh") * lax.axis_size("core") + lax.axis_index("core")
    micros, img_mb, patch_count, width = visual_fragments.shape
    tok_rows = img_mb * patch_count
    plane = stages * around
    scale = score_scaling[0]
    shift = score_shift[0]
    texts_dev = caption_outputs.shape[0]
    prior_dev = earlier_averaged.shape[0]

    up = widening_kernel[0].T
    down = narrowing_kernel[0]
    both = jnp.stack([up, down])
    both = jnp.concatenate([both, swap(both, "yh")], axis=1)
    units = both.shape[1]
    padded = -(-units // 8) * 8
    both = jnp.pad(both, ((0, 0), (0, padded - units), (0, 0)))
    up_own = lax.all_gather(both[0], "z", axis=0, tiled=True)
    down_own = lax.all_gather(both[1], "z", axis=0, tiled=True)

    text_own = unit_rows(caption_outputs)
    prior_own = unit_rows(earlier_averaged)
    texts = share_rows(text_own, "z", depth).reshape(depth * texts_dev, width)
    priors = share_rows(prior_own, PLANE, plane).reshape(plane * prior_dev, width)
    labels = lax.dynamic_index_in_dim(
        match_targets.reshape(stages, depth, around, img_mb + prior_dev), z_id, 1, keepdims=False
    )
    columns = (
        ((stage_id * depth + jnp.arange(depth, dtype=jnp.int32)) * around + around_id) * texts_dev
    )[:, None] + jnp.arange(texts_dev, dtype=jnp.int32)[None, :]
    columns = columns.reshape(-1)
    grid = pair_weights(priors, texts, labels[:, :, img_mb:].reshape(-1), columns, scale, shift)
    prior_part = jnp.dot(grid, texts, preferred_element_type=jnp.float32).astype(jnp.bfloat16)
    prior_part = lax.all_to_all(prior_part.reshape(plane, prior_dev, width), PLANE, 0, 0)
    prior_grad = jnp.sum(prior_part.astype(jnp.float32), axis=0)
    text_early = across(grid, priors)
    up_own, down_own, prior_grad, text_early = lax.optimization_barrier((up_own, down_own, prior_grad, text_early))
    weights = (up_own, down_own, swap(up_own, "core"), swap(down_own, "core"))

    groups = micros // GROUP
    panels = visual_fragments.reshape(groups, GROUP * tok_rows, width)
    first = (stage_id == 0).astype(jnp.int32).reshape(1)
    ring = [(source, (source + 1) % stages) for source in range(stages)]
    last = STAGE_GAP * (stages - 1)
    sent = []
    pooled = []
    for slot in range(groups + last):
        pick = min(slot, groups - 1)
        if slot < STAGE_GAP:
            take, carried = "panel", panels[pick]
        else:
            take, carried = ("either" if slot < groups else "carried"), sent[slot - STAGE_GAP]
        moved, mean = stage(first, panels, pick, carried, weights, GROUP * img_mb, take)
        if slot >= last:
            pooled.append(mean)
        sent.append(lax.ppermute(moved, "pipe", ring) if slot < last + groups - STAGE_GAP else None)
    tower_own = unit_rows(jnp.concatenate(pooled, axis=0))

    tower = share_rows(tower_own, PLANE, plane).reshape(stages, around, micros, width)[stages - 1]
    tower = tower.reshape(around * micros, width)
    tower_labels = labels[:, :, 0].T.reshape(-1)
    tower_grid = pair_weights(tower, texts, tower_labels, columns, scale, shift)
    tower_part = jnp.dot(tower_grid, texts, preferred_element_type=jnp.float32).astype(jnp.bfloat16)
    tower_part = tower_part.reshape(around, micros, width).transpose(1, 0, 2).reshape(plane, img_mb, width)
    tower_part = lax.all_to_all(tower_part, PLANE, 0, 0)
    tower_grad = jnp.sum(tower_part.astype(jnp.float32), axis=0)
    text_part = text_early + across(tower_grid, tower)
    text_part = text_part.astype(jnp.bfloat16).reshape(depth, texts_dev, width)
    text_grad = jnp.sum(lax.all_to_all(text_part, "z", 0, 0).astype(jnp.float32), axis=0)
    return jnp.concatenate([tower_grad, prior_grad], axis=0), text_grad


def solution(mesh):
    sizes = dict(mesh.shape)
    stages = sizes["pipe"]
    fine = Mesh(mesh.devices.reshape(stages, sizes["dp"] // 4, 2, 2), EVERY)
    data = ("z", "yh", "core")
    placed = (
        P(None, data, None, None),
        P("pipe", None, data),
        P("pipe", data, None),
        P(EVERY, None),
        P(EVERY, None),
        P(),
        P(),
        P(),
    )
    return jax.shard_map(
        body,
        mesh=fine,
        in_specs=placed,
        out_specs=(P(EVERY, None), P(EVERY, None)),
        check_vma=False,
    )
```

time: 1400 us -> 491 us (0.35)
  waiting for transfers between devices: 1210 us -> 170 us
  Pallas kernels: 0 us -> 138 us
  starting transfers between devices: 33 us -> 137 us
  matrix products: 49.4 us -> 3.54 us
  local copies, waits for them, and re-layouts: 40.1 us -> 12.7 us
  blocking collectives: 22.1 us -> 0 us
  other arithmetic: 22.9 us -> 5.35 us
    unnamed x7 -> x2, waiting for transfers between devices: 621 us -> 0.71 us
    all_gather x3 -> x2, waiting for transfers between devices: 473 us -> 68.8 us  [the longest x1 68.7 us: body(): up_own = lax.all_gather(both[0], 'z', axis=0, tiled=True)]
    pallas_call x0 -> x22, Pallas kernels: none -> 138 us  [stage(): pl.pallas_call(functools.partial(stage_kernel, take=take, wide=wide, narr...]
    ppermute x15 -> x23, waiting for transfers between devices: 117 us -> 8.72 us  [the longest x3 8.66 us: swap(): return lax.ppermute(value, axis, [(0, 1), (1, 0)])]
    all_to_all x0 -> x6, waiting for transfers between devices: none -> 92 us  [the longest x3 50.5 us: share_rows(): return lax.all_to_all(copies, axes, 0, 0)]
    all_to_all x0 -> x6, starting transfers between devices: none -> 59.4 us  [the longest x3 44 us: share_rows(): return lax.all_to_all(copies, axes, 0, 0)]
    dot_general x11 -> x6, matrix products: 49.4 us -> 3.54 us  [the longest x2 1.47 us: across(): lax.dot_general(grid, other, (((0,), (0,)), ((), ())), preferred_element_...]
    ppermute x15 -> x23, starting transfers between devices: 32.8 us -> 77.9 us  [the longest x20 58.7 us: body(): lax.ppermute(moved, 'pipe', ring)]
  transfers between devices with their start and end apart: 20 -> 31, of which waited for: 20 -> 10; matrix products, arithmetic and copies ran while one was open for 2% -> 2% of each run, Pallas kernels for 0% -> 26%
where the time goes in v1:
time: 491 us; the launch traced here: 483 us
  waiting for transfers between devices  170 us (35%)
  Pallas kernels  138 us (28%)
  starting transfers between devices  137 us (28%)
  between operations  16 us (3%)
  local copies, waits for them, and re-layouts  12.7 us (3%)
  other arithmetic  5.35 us (1%)
    pallas_call x22, Pallas kernels, stage(): pl.pallas_call(functools.partial(stage_kernel, take=take, wide=wide, narr...  138 us
    all_gather x1, waiting for transfers between devices, body(): up_own = lax.all_gather(both[0], 'z', axis=0, tiled=True)  68.7 us
    ppermute x20, starting transfers between devices, body(): lax.ppermute(moved, 'pipe', ring)  58.7 us
    all_to_all x3, waiting for transfers between devices, share_rows(): return lax.all_to_all(copies, axes, 0, 0)  50.5 us
    all_to_all x3, starting transfers between devices, share_rows(): return lax.all_to_all(copies, axes, 0, 0)  44 us
    all_to_all x1, waiting for transfers between devices, body(): lax.all_to_all(text_part, 'z', 0, 0).astype(jnp.float32)  24.3 us
    ppermute x3, starting transfers between devices, swap(): return lax.ppermute(value, axis, [(0, 1), (1, 0)])  19.2 us
    all_to_all x1, waiting for transfers between devices, body(): lax.all_to_all(prior_part.reshape(plane, prior_dev, width), PLANE, 0, 0)  11.1 us
  transfers between devices with their start and end apart: 31, of which 10 were waited for; matrix products, arithmetic and copies ran while one was open for 2% of the time, Pallas kernels for 26%

profile of v1, /device:TPU:1, one launch (start us, length us, event | category | flops | bytes accessed | tf_op | source)
XLA Modules:
  0.0 483.1 jit_solution(2888019804245751011)
XLA Ops:
  20.4 16.1 %all-to-all-start.1 = ((bf16[16,9,1152]{2,1,0:T(8,128)(2,1)}), bf16[16,9,1152]{2,1,0:T(8,128)(2,1)S(1)}, u32[]{:S(2)}, u32[]{:S(2)}) async-start(bf16[16,9,1152]{2,1,0:T(8,128)(2,1)} %broadcast_in_dim.7), calls=%async_computation.1 | async-start | bytes 1179648 | tf_op jit(solution)/shard_map/all_to_all | solution.py:24
  36.7 28.5 %all-to-all-done.1 = bf16[16,9,1152]{2,1,0:T(8,128)(2,1)S(1)} async-done(((bf16[16,9,1152]{2,1,0:T(8,128)(2,1)}), bf16[16,9,1152]{2,1,0:T(8,128)(2,1)S(1)}, u32[]{:S(2)}, u32[]{:S(2)}) %all-to-all-start.1) | async-done | bytes 331808 | tf_op jit(solution)/shard_map/all_to_all | solution.py:24
  66.1 15.5 %all-to-all-start = ((bf16[32,8,1152]{2,1,0:T(8,128)(2,1)}), bf16[32,8,1152]{2,1,0:T(8,128)(2,1)S(1)}, u32[]{:S(2)}, u32[]{:S(2)}) async-start(bf16[32,8,1152]{2,1,0:T(8,128)(2,1)} %broadcast_in_dim.6), calls=%async_computation | async-start | bytes 1179648 | tf_op jit(solution)/shard_map/all_to_all | solution.py:24
  83.8 10.0 %all-to-all-done = bf16[32,8,1152]{2,1,0:T(8,128)(2,1)S(1)} async-done(((bf16[32,8,1152]{2,1,0:T(8,128)(2,1)}), bf16[32,8,1152]{2,1,0:T(8,128)(2,1)S(1)}, u32[]{:S(2)}, u32[]{:S(2)}) %all-to-all-start) | async-done | bytes 589856 | tf_op jit(solution)/shard_map/all_to_all | solution.py:24
  100.7 11.1 %all-to-all-done.2 = bf16[32,8,1152]{2,1,0:T(8,128)(2,1)S(1)} async-done(((bf16[32,8,1152]{2,1,0:T(8,128)(2,1)}), bf16[32,8,1152]{2,1,0:T(8,128)(2,1)S(1)}, u32[]{:S(2)}, u32[]{:S(2)}) %all-to-all-start.2) | async-done | bytes 589856 | tf_op jit(solution)/shard_map/all_to_all | solution.py:182
  111.9 68.7 %all-gather.5.cloned.1.call-done = bf16[1,1152,1152]{2,1,0:T(8,128)(2,1)} async-done(((bf16[1,72,1152]{2,1,0:T(8,128)(2,1)}), bf16[1,1152,1152]{2,1,0:T(8,128)(2,1)}) %all-gather.5.cloned.1.call-update) | async-done | bytes 2654224 | tf_op jit(solution)/shard_map/all_gather | solution.py:166
  180.7 11.6 %collective-permute-start.1 = (bf16[1152,1152]{1,0:T(8,128)(2,1)}, bf16[1152,1152]{1,0:T(8,128)(2,1)S(1)}, u32[]{:S(2)}, u32[]{:S(2)}) collective-permute-start(bf16[1152,1152]{1,0:T(8,128)(2,1)} %bitcast.77), channel_id=1, source_target_pairs={{0,1},{1,0},{2,3},{3,2},{4,5},{5,4},{6,7},{7,6},{8,9},{9,8},{10,11... | collective-permute-start | bytes 7962632 | tf_op jit(solution)/shard_map/ppermute | solution.py:28
  205.8 6.6 %stage.22 = (bf16[64,1152]{1,0:T(8,128)(2,1)S(1)}, f32[1,1152]{1,0:T(1,128)}) custom-call(s32[1]{0:T(128)} %bitcast.4.first_ref, bf16[8,64,1152]{2,1,0:T(8,128)(2,1)S(1)} %bitcast.100, bf16[64,1152]{1,0:T(8,128)(2,1)S(1)} %get-tuple-element.67.carried_ref, bf16[1152,1152]{1,0:T(8,128)(2,1)S(1)} %bitcast.78, bf16[1152,1152]{1,0:T(8,128)(2,1)S(1)} %bitcast.55, ...), custom_call_target="tpu_custom_call" | custom-call | flops 679477248 | bytes 10616832 | tf_op jit(solution)/shard_map/stage/pallas_call | solution.py:82
  215.4 6.4 %stage.30 = (bf16[64,1152]{1,0:T(8,128)(2,1)S(1)}, f32[1,1152]{1,0:T(1,128)}) custom-call(s32[1]{0:T(128)} %bitcast.4.first_ref, bf16[8,64,1152]{2,1,0:T(8,128)(2,1)S(1)} %bitcast.101, bf16[64,1152]{1,0:T(8,128)(2,1)S(1)} %get-tuple-element.66.carried_ref, bf16[1152,1152]{1,0:T(8,128)(2,1)S(1)} %bitcast.79, bf16[1152,1152]{1,0:T(8,128)(2,1)S(1)} %bitcast.56, ...), custom_call_target="tpu_custom_call" | custom-call | flops 679477248 | bytes 10616832 | tf_op jit(solution)/shard_map/stage/pallas_call | solution.py:82
  225.0 6.4 %stage.23 = (bf16[64,1152]{1,0:T(8,128)(2,1)S(1)}, f32[1,1152]{1,0:T(1,128)}) custom-call(s32[1]{0:T(128)} %bitcast.4.first_ref, bf16[8,64,1152]{2,1,0:T(8,128)(2,1)S(1)} %bitcast.102, bf16[64,1152]{1,0:T(8,128)(2,1)S(1)} %collective-permute-done.3.carried_ref, bf16[1152,1152]{1,0:T(8,128)(2,1)S(1)} %bitcast.80, bf16[1152,1152]{1,0:T(8,128)(2,1)S(1)} %bitcast.57, ...), custom_call_target="tpu_custom_call" | custom-call | flops 679477248 | bytes 10616832 | tf_op jit(solution)/shard_map/stage/pallas_call | solution.py:82
  234.2 6.4 %stage.31 = (bf16[64,1152]{1,0:T(8,128)(2,1)S(1)}, f32[1,1152]{1,0:T(1,128)}) custom-call(s32[1]{0:T(128)} %bitcast.4.first_ref, bf16[8,64,1152]{2,1,0:T(8,128)(2,1)S(1)} %bitcast.103, bf16[64,1152]{1,0:T(8,128)(2,1)S(1)} %collective-permute-done.10.carried_ref, bf16[1152,1152]{1,0:T(8,128)(2,1)S(1)} %bitcast.81, bf16[1152,1152]{1,0:T(8,128)(2,1)S(1)} %bitcast.58, ...), custom_call_target="tpu_custom_call" | custom-call | flops 679477248 | bytes 10616832 | tf_op jit(solution)/shard_map/stage/pallas_call | solution.py:82
  243.9 6.4 %stage.24 = (bf16[64,1152]{1,0:T(8,128)(2,1)S(1)}, f32[1,1152]{1,0:T(1,128)}) custom-call(s32[1]{0:T(128)} %bitcast.4.first_ref, bf16[8,64,1152]{2,1,0:T(8,128)(2,1)S(1)} %bitcast.104, bf16[64,1152]{1,0:T(8,128)(2,1)S(1)} %collective-permute-done.4.carried_ref, bf16[1152,1152]{1,0:T(8,128)(2,1)S(1)} %bitcast.82, bf16[1152,1152]{1,0:T(8,128)(2,1)S(1)} %bitcast.59, ...), custom_call_target="tpu_custom_call" | custom-call | flops 679477248 | bytes 10616832 | tf_op jit(solution)/shard_map/stage/pallas_call | solution.py:82
  253.3 6.4 %stage.32 = (bf16[64,1152]{1,0:T(8,128)(2,1)S(1)}, f32[1,1152]{1,0:T(1,128)}) custom-call(s32[1]{0:T(128)} %bitcast.4.first_ref, bf16[8,64,1152]{2,1,0:T(8,128)(2,1)S(1)} %bitcast.105, bf16[64,1152]{1,0:T(8,128)(2,1)S(1)} %collective-permute-done.11.carried_ref, bf16[1152,1152]{1,0:T(8,128)(2,1)S(1)} %bitcast.83, bf16[1152,1152]{1,0:T(8,128)(2,1)S(1)} %bitcast.60, ...), custom_call_target="tpu_custom_call" | custom-call | flops 679477248 | bytes 10616832 | tf_op jit(solution)/shard_map/stage/pallas_call | solution.py:82
  262.8 6.4 %stage.25 = (bf16[64,1152]{1,0:T(8,128)(2,1)S(1)}, f32[1,1152]{1,0:T(1,128)}) custom-call(s32[1]{0:T(128)} %bitcast.4.first_ref, bf16[8,64,1152]{2,1,0:T(8,128)(2,1)S(1)} %bitcast.106, bf16[64,1152]{1,0:T(8,128)(2,1)S(1)} %collective-permute-done.5.carried_ref, bf16[1152,1152]{1,0:T(8,128)(2,1)S(1)} %bitcast.84, bf16[1152,1152]{1,0:T(8,128)(2,1)S(1)} %bitcast.61, ...), custom_call_target="tpu_custom_call" | custom-call | flops 679477248 | bytes 10616832 | tf_op jit(solution)/shard_map/stage/pallas_call | solution.py:82
  272.1 6.4 %stage.33 = (bf16[64,1152]{1,0:T(8,128)(2,1)S(1)}, f32[1,1152]{1,0:T(1,128)}) custom-call(s32[1]{0:T(128)} %bitcast.4.first_ref, bf16[8,64,1152]{2,1,0:T(8,128)(2,1)S(1)} %bitcast.107, bf16[64,1152]{1,0:T(8,128)(2,1)S(1)} %collective-permute-done.12.carried_ref, bf16[1152,1152]{1,0:T(8,128)(2,1)S(1)} %bitcast.85, bf16[1152,1152]{1,0:T(8,128)(2,1)S(1)} %bitcast.62, ...), custom_call_target="tpu_custom_call" | custom-call | flops 679477248 | bytes 10616832 | tf_op jit(solution)/shard_map/stage/pallas_call | solution.py:82
  280.6 6.4 %stage.26 = (bf16[64,1152]{1,0:T(8,128)(2,1)S(1)}, f32[1,1152]{1,0:T(1,128)}) custom-call(s32[1]{0:T(128)} %bitcast.4.first_ref, bf16[8,64,1152]{2,1,0:T(8,128)(2,1)S(1)} %bitcast.108, bf16[64,1152]{1,0:T(8,128)(2,1)S(1)} %collective-permute-done.6.carried_ref, bf16[1152,1152]{1,0:T(8,128)(2,1)S(1)} %bitcast.86, bf16[1152,1152]{1,0:T(8,128)(2,1)S(1)} %bitcast.63, ...), custom_call_target="tpu_custom_call" | custom-call | flops 679477248 | bytes 10616832 | tf_op jit(solution)/shard_map/stage/pallas_call | solution.py:82
  299.9 6.4 %stage.27 = (bf16[64,1152]{1,0:T(8,128)(2,1)S(1)}, f32[1,1152]{1,0:T(1,128)}) custom-call(s32[1]{0:T(128)} %bitcast.4.first_ref, bf16[8,64,1152]{2,1,0:T(8,128)(2,1)S(1)} %bitcast.110, bf16[64,1152]{1,0:T(8,128)(2,1)S(1)} %collective-permute-done.7.carried_ref, bf16[1152,1152]{1,0:T(8,128)(2,1)S(1)} %bitcast.88, bf16[1152,1152]{1,0:T(8,128)(2,1)S(1)} %bitcast.65, ...), custom_call_target="tpu_custom_call" | custom-call | flops 679477248 | bytes 10616832 | tf_op jit(solution)/shard_map/stage/pallas_call | solution.py:82
  309.1 6.4 %stage.35 = (bf16[64,1152]{1,0:T(8,128)(2,1)S(1)}, f32[1,1152]{1,0:T(1,128)}) custom-call(s32[1]{0:T(128)} %bitcast.4.first_ref, bf16[8,64,1152]{2,1,0:T(8,128)(2,1)S(1)} %bitcast.111, bf16[64,1152]{1,0:T(8,128)(2,1)S(1)} %collective-permute-done.14.carried_ref, bf16[1152,1152]{1,0:T(8,128)(2,1)S(1)} %bitcast.89, bf16[1152,1152]{1,0:T(8,128)(2,1)S(1)} %bitcast.66, ...), custom_call_target="tpu_custom_call" | custom-call | flops 679477248 | bytes 10616832 | tf_op jit(solution)/shard_map/stage/pallas_call | solution.py:82
  390.0 6.5 %stage.42 = (bf16[64,1152]{1,0:T(8,128)(2,1)}, f32[1,1152]{1,0:T(1,128)S(1)}) custom-call(s32[1]{0:T(128)} %bitcast.4.first_ref, bf16[8,64,1152]{2,1,0:T(8,128)(2,1)S(1)} %bitcast.120, bf16[64,1152]{1,0:T(8,128)(2,1)S(1)} %collective-permute-done.21.carried_ref, bf16[1152,1152]{1,0:T(8,128)(2,1)S(1)} %bitcast.98, bf16[1152,1152]{1,0:T(8,128)(2,1)S(1)} %bitcast.75, ...), custom_call_target="tpu_custom_call" | custom-call | flops 679477248 | bytes 10616832 | tf_op jit(solution)/shard_map/stage/pallas_call | solution.py:82
  396.5 6.5 %stage.43 = (bf16[64,1152]{1,0:T(8,128)(2,1)}, f32[1,1152]{1,0:T(1,128)S(1)}) custom-call(s32[1]{0:T(128)} %bitcast.4.first_ref, bf16[8,64,1152]{2,1,0:T(8,128)(2,1)S(1)} %bitcast.121, bf16[64,1152]{1,0:T(8,128)(2,1)S(1)} %collective-permute-done.22.carried_ref, bf16[1152,1152]{1,0:T(8,128)(2,1)S(1)} %bitcast.99, bf16[1152,1152]{1,0:T(8,128)(2,1)S(1)} %bitcast.76, ...), custom_call_target="tpu_custom_call" | custom-call | flops 679477248 | bytes 10616832 | tf_op jit(solution)/shard_map/stage/pallas_call | solution.py:82
  404.1 12.4 %all-to-all-start.3 = ((bf16[32,8,1152]{2,1,0:T(8,128)(2,1)}), bf16[32,8,1152]{2,1,0:T(8,128)(2,1)S(1)}, u32[]{:S(2)}, u32[]{:S(2)}) async-start(bf16[32,8,1152]{2,1,0:T(8,128)(2,1)} %broadcast_in_dim.8), calls=%async_computation.3 | async-start | bytes 1179648 | tf_op jit(solution)/shard_map/all_to_all | solution.py:24
  416.7 12.0 %all-to-all-done.3 = bf16[32,8,1152]{2,1,0:T(8,128)(2,1)S(1)} async-done(((bf16[32,8,1152]{2,1,0:T(8,128)(2,1)}), bf16[32,8,1152]{2,1,0:T(8,128)(2,1)S(1)}, u32[]{:S(2)}, u32[]{:S(2)}) %all-to-all-start.3) | async-done | bytes 589856 | tf_op jit(solution)/shard_map/all_to_all | solution.py:24
  443.1 7.2 %all-to-all-start.5 = ((bf16[16,9,1152]{2,1,0:T(8,128)(2,1)}), bf16[16,9,1152]{2,1,0:T(8,128)(2,1)S(1)}, u32[]{:S(2)}, u32[]{:S(2)}) async-start(bf16[16,9,1152]{2,1,0:T(8,128)(2,1)} %reshape.163), calls=%async_computation.5 | async-start | bytes 1179648 | tf_op jit(solution)/shard_map/all_to_all | solution.py:217
  451.2 24.3 %all-to-all-done.5 = bf16[16,9,1152]{2,1,0:T(8,128)(2,1)S(1)} async-done(((bf16[16,9,1152]{2,1,0:T(8,128)(2,1)}), bf16[16,9,1152]{2,1,0:T(8,128)(2,1)S(1)}, u32[]{:S(2)}, u32[]{:S(2)}) %all-to-all-start.5) | async-done | bytes 331808 | tf_op jit(solution)/shard_map/all_to_all | solution.py:217
  (123 shorter events, 165.9 us)
Async XLA Ops:
  7.2 104.8 %all-gather.7.cloned.1.call-start = ((), (), s32[]{:S(2)}) async-start(), calls=%async_computation.7 | async-start | bytes 2820096 | tf_op jit(solution)/shard_map/all_gather | solution.py:167
  18.6 162.1 %all-gather.5.cloned.1.call-start = ((), (), s32[]{:S(2)}) async-start(), calls=%async_computation.6 | async-start | bytes 2820096 | tf_op jit(solution)/shard_map/all_gather | solution.py:166
  20.4 44.8 %all-to-all-start.1 = ((bf16[16,9,1152]{2,1,0:T(8,128)(2,1)}), bf16[16,9,1152]{2,1,0:T(8,128)(2,1)S(1)}, u32[]{:S(2)}, u32[]{:S(2)}) async-start(bf16[16,9,1152]{2,1,0:T(8,128)(2,1)} %broadcast_in_dim.7), calls=%async_computation.1 | async-start | bytes 1179648 | tf_op jit(solution)/shard_map/all_to_all | solution.py:24
  66.1 27.7 %all-to-all-start = ((bf16[32,8,1152]{2,1,0:T(8,128)(2,1)}), bf16[32,8,1152]{2,1,0:T(8,128)(2,1)S(1)}, u32[]{:S(2)}, u32[]{:S(2)}) async-start(bf16[32,8,1152]{2,1,0:T(8,128)(2,1)} %broadcast_in_dim.6), calls=%async_computation | async-start | bytes 1179648 | tf_op jit(solution)/shard_map/all_to_all | solution.py:24
  95.4 16.4 %all-to-all-start.2 = ((bf16[32,8,1152]{2,1,0:T(8,128)(2,1)}), bf16[32,8,1152]{2,1,0:T(8,128)(2,1)S(1)}, u32[]{:S(2)}, u32[]{:S(2)}) async-start(bf16[32,8,1152]{2,1,0:T(8,128)(2,1)} %fusion), calls=%async_computation.2 | async-start | bytes 1179648 | tf_op jit(solution)/shard_map/all_to_all | solution.py:182
  180.7 16.4 %collective-permute-start.1 = (bf16[1152,1152]{1,0:T(8,128)(2,1)}, bf16[1152,1152]{1,0:T(8,128)(2,1)S(1)}, u32[]{:S(2)}, u32[]{:S(2)}) collective-permute-start(bf16[1152,1152]{1,0:T(8,128)(2,1)} %bitcast.77), channel_id=1, source_target_pairs={{0,1},{1,0},{2,3},{3,2},{4,5},{5,4},{6,7},{7,6},{8,9},{9,8},{10,11... | collective-permute-start | bytes 7962632 | tf_op jit(solution)/shard_map/ppermute | solution.py:28
  212.3 12.6 %collective-permute-start.3 = (bf16[64,1152]{1,0:T(8,128)(2,1)S(1)}, bf16[64,1152]{1,0:T(8,128)(2,1)S(1)}, u32[]{:S(2)}, u32[]{:S(2)}) collective-permute-start(bf16[64,1152]{1,0:T(8,128)(2,1)S(1)} %get-tuple-element.36), channel_id=1, source_target_pairs={{0,64},{64,128},{128,192},{192,256},{256,320},{320,384},{384,448},... | collective-permute-start | bytes 442376 | tf_op jit(solution)/shard_map/ppermute | solution.py:204
  221.9 12.3 %collective-permute-start.10 = (bf16[64,1152]{1,0:T(8,128)(2,1)S(1)}, bf16[64,1152]{1,0:T(8,128)(2,1)S(1)}, u32[]{:S(2)}, u32[]{:S(2)}) collective-permute-start(bf16[64,1152]{1,0:T(8,128)(2,1)S(1)} %get-tuple-element.44), channel_id=1, source_target_pairs={{0,64},{64,128},{128,192},{192,256},{256,320},{320,384},{384,448},... | collective-permute-start | bytes 442376 | tf_op jit(solution)/shard_map/ppermute | solution.py:204
  231.4 12.5 %collective-permute-start.4 = (bf16[64,1152]{1,0:T(8,128)(2,1)S(1)}, bf16[64,1152]{1,0:T(8,128)(2,1)S(1)}, u32[]{:S(2)}, u32[]{:S(2)}) collective-permute-start(bf16[64,1152]{1,0:T(8,128)(2,1)S(1)} %get-tuple-element.37), channel_id=1, source_target_pairs={{0,64},{64,128},{128,192},{192,256},{256,320},{320,384},{384,448},... | collective-permute-start | bytes 442376 | tf_op jit(solution)/shard_map/ppermute | solution.py:204
  240.6 12.6 %collective-permute-start.11 = (bf16[64,1152]{1,0:T(8,128)(2,1)S(1)}, bf16[64,1152]{1,0:T(8,128)(2,1)S(1)}, u32[]{:S(2)}, u32[]{:S(2)}) collective-permute-start(bf16[64,1152]{1,0:T(8,128)(2,1)S(1)} %get-tuple-element.45), channel_id=1, source_target_pairs={{0,64},{64,128},{128,192},{192,256},{256,320},{320,384},{384,448},... | collective-permute-start | bytes 442376 | tf_op jit(solution)/shard_map/ppermute | solution.py:204
  250.3 12.5 %collective-permute-start.5 = (bf16[64,1152]{1,0:T(8,128)(2,1)S(1)}, bf16[64,1152]{1,0:T(8,128)(2,1)S(1)}, u32[]{:S(2)}, u32[]{:S(2)}) collective-permute-start(bf16[64,1152]{1,0:T(8,128)(2,1)S(1)} %get-tuple-element.38), channel_id=1, source_target_pairs={{0,64},{64,128},{128,192},{192,256},{256,320},{320,384},{384,448},... | collective-permute-start | bytes 442376 | tf_op jit(solution)/shard_map/ppermute | solution.py:204
  259.7 12.3 %collective-permute-start.12 = (bf16[64,1152]{1,0:T(8,128)(2,1)S(1)}, bf16[64,1152]{1,0:T(8,128)(2,1)S(1)}, u32[]{:S(2)}, u32[]{:S(2)}) collective-permute-start(bf16[64,1152]{1,0:T(8,128)(2,1)S(1)} %get-tuple-element.46), channel_id=1, source_target_pairs={{0,64},{64,128},{128,192},{192,256},{256,320},{320,384},{384,448},... | collective-permute-start | bytes 442376 | tf_op jit(solution)/shard_map/ppermute | solution.py:204
  278.5 11.9 %collective-permute-start.13 = (bf16[64,1152]{1,0:T(8,128)(2,1)S(1)}, bf16[64,1152]{1,0:T(8,128)(2,1)S(1)}, u32[]{:S(2)}, u32[]{:S(2)}) collective-permute-start(bf16[64,1152]{1,0:T(8,128)(2,1)S(1)} %get-tuple-element.47), channel_id=1, source_target_pairs={{0,64},{64,128},{128,192},{192,256},{256,320},{320,384},{384,448},... | collective-permute-start | bytes 442376 | tf_op jit(solution)/shard_map/ppermute | solution.py:204
  287.1 12.8 %collective-permute-start.7 = (bf16[64,1152]{1,0:T(8,128)(2,1)S(1)}, bf16[64,1152]{1,0:T(8,128)(2,1)S(1)}, u32[]{:S(2)}, u32[]{:S(2)}) collective-permute-start(bf16[64,1152]{1,0:T(8,128)(2,1)S(1)} %get-tuple-element.40), channel_id=1, source_target_pairs={{0,64},{64,128},{128,192},{192,256},{256,320},{320,384},{384,448},... | collective-permute-start | bytes 442376 | tf_op jit(solution)/shard_map/ppermute | solution.py:204
  296.8 12.3 %collective-permute-start.14 = (bf16[64,1152]{1,0:T(8,128)(2,1)S(1)}, bf16[64,1152]{1,0:T(8,128)(2,1)S(1)}, u32[]{:S(2)}, u32[]{:S(2)}) collective-permute-start(bf16[64,1152]{1,0:T(8,128)(2,1)S(1)} %get-tuple-element.48), channel_id=1, source_target_pairs={{0,64},{64,128},{128,192},{192,256},{256,320},{320,384},{384,448},... | collective-permute-start | bytes 442376 | tf_op jit(solution)/shard_map/ppermute | solution.py:204
  306.3 12.5 %collective-permute-start.8 = (bf16[64,1152]{1,0:T(8,128)(2,1)S(1)}, bf16[64,1152]{1,0:T(8,128)(2,1)S(1)}, u32[]{:S(2)}, u32[]{:S(2)}) collective-permute-start(bf16[64,1152]{1,0:T(8,128)(2,1)S(1)} %get-tuple-element.41), channel_id=1, source_target_pairs={{0,64},{64,128},{128,192},{192,256},{256,320},{320,384},{384,448},... | collective-permute-start | bytes 442376 | tf_op jit(solution)/shard_map/ppermute | solution.py:204
  315.5 12.6 %collective-permute-start.15 = (bf16[64,1152]{1,0:T(8,128)(2,1)S(1)}, bf16[64,1152]{1,0:T(8,128)(2,1)S(1)}, u32[]{:S(2)}, u32[]{:S(2)}) collective-permute-start(bf16[64,1152]{1,0:T(8,128)(2,1)S(1)} %get-tuple-element.49), channel_id=1, source_target_pairs={{0,64},{64,128},{128,192},{192,256},{256,320},{320,384},{384,448},... | collective-permute-start | bytes 442376 | tf_op jit(solution)/shard_map/ppermute | solution.py:204
  325.2 12.5 %collective-permute-start.9 = (bf16[64,1152]{1,0:T(8,128)(2,1)S(1)}, bf16[64,1152]{1,0:T(8,128)(2,1)S(1)}, u32[]{:S(2)}, u32[]{:S(2)}) collective-permute-start(bf16[64,1152]{1,0:T(8,128)(2,1)S(1)} %get-tuple-element.42), channel_id=1, source_target_pairs={{0,64},{64,128},{128,192},{192,256},{256,320},{320,384},{384,448},... | collective-permute-start | bytes 442376 | tf_op jit(solution)/shard_map/ppermute | solution.py:204
  334.6 11.8 %collective-permute-start.16 = (bf16[64,1152]{1,0:T(8,128)(2,1)S(1)}, bf16[64,1152]{1,0:T(8,128)(2,1)S(1)}, u32[]{:S(2)}, u32[]{:S(2)}) collective-permute-start(bf16[64,1152]{1,0:T(8,128)(2,1)S(1)} %get-tuple-element.50), channel_id=1, source_target_pairs={{0,64},{64,128},{128,192},{192,256},{256,320},{320,384},{384,448},... | collective-permute-start | bytes 442376 | tf_op jit(solution)/shard_map/ppermute | solution.py:204
  360.2 12.1 %collective-permute-start.19 = (bf16[64,1152]{1,0:T(8,128)(2,1)S(1)}, bf16[64,1152]{1,0:T(8,128)(2,1)S(1)}, u32[]{:S(2)}, u32[]{:S(2)}) collective-permute-start(bf16[64,1152]{1,0:T(8,128)(2,1)S(1)} %get-tuple-element.56), channel_id=1, source_target_pairs={{0,64},{64,128},{128,192},{192,256},{256,320},{320,384},{384,448},... | collective-permute-start | bytes 442376 | tf_op jit(solution)/shard_map/ppermute | solution.py:204
  369.1 11.8 %collective-permute-start.20 = (bf16[64,1152]{1,0:T(8,128)(2,1)S(1)}, bf16[64,1152]{1,0:T(8,128)(2,1)S(1)}, u32[]{:S(2)}, u32[]{:S(2)}) collective-permute-start(bf16[64,1152]{1,0:T(8,128)(2,1)S(1)} %get-tuple-element.58), channel_id=1, source_target_pairs={{0,64},{64,128},{128,192},{192,256},{256,320},{320,384},{384,448},... | collective-permute-start | bytes 442376 | tf_op jit(solution)/shard_map/ppermute | solution.py:204
  378.1 11.9 %collective-permute-start.21 = (bf16[64,1152]{1,0:T(8,128)(2,1)S(1)}, bf16[64,1152]{1,0:T(8,128)(2,1)S(1)}, u32[]{:S(2)}, u32[]{:S(2)}) collective-permute-start(bf16[64,1152]{1,0:T(8,128)(2,1)S(1)} %get-tuple-element.60), channel_id=1, source_target_pairs={{0,64},{64,128},{128,192},{192,256},{256,320},{320,384},{384,448},... | collective-permute-start | bytes 442376 | tf_op jit(solution)/shard_map/ppermute | solution.py:204
  404.1 24.6 %all-to-all-start.3 = ((bf16[32,8,1152]{2,1,0:T(8,128)(2,1)}), bf16[32,8,1152]{2,1,0:T(8,128)(2,1)S(1)}, u32[]{:S(2)}, u32[]{:S(2)}) async-start(bf16[32,8,1152]{2,1,0:T(8,128)(2,1)} %broadcast_in_dim.8), calls=%async_computation.3 | async-start | bytes 1179648 | tf_op jit(solution)/shard_map/all_to_all | solution.py:24
  443.1 32.5 %all-to-all-start.5 = ((bf16[16,9,1152]{2,1,0:T(8,128)(2,1)}), bf16[16,9,1152]{2,1,0:T(8,128)(2,1)S(1)}, u32[]{:S(2)}, u32[]{:S(2)}) async-start(bf16[16,9,1152]{2,1,0:T(8,128)(2,1)} %reshape.163), calls=%async_computation.5 | async-start | bytes 1179648 | tf_op jit(solution)/shard_map/all_to_all | solution.py:217
  (15 other events, 182.1 us)
Sparse Core Ops, SparseCore 0:
  18.7 90.2 all-gather.6
  111.1 69.5 all-gather.4
